TPU v7x, 32 devices: a whole 2x2x4 slice. The times are simulated.
32 devices in a mesh: tensor: 2 (over x), expert: 16 (over z, y, core).
Axes of the slice: x: 2, y: 2, z: 4, core: 2. Of those that a mesh axis runs over, the one named last changes fastest.
Arguments:
- out_grad: bfloat16 [16, 32, 4096], P('expert', 'tensor'), may hold values from -6 to 6
- norm_input: bfloat16 [16, 32, 4096], P('expert', 'tensor'), may hold values from -24 to 24
- norm_gain: float32 [4096], replicated, may hold values from 0.3 to 3
- routes: int32 [16, 32, 8], P('expert'), may hold values from 0 to 15, all different within a row; in each aligned block of 32 rows (0 to 31, 32 to 63, ..., all dimensions but the last counted through in order) at most 32 rows name the same one
- route_weight: float32 [16, 32, 8], P('expert'), may hold values from 0.05 to 0.25
- gate_saved: bfloat16 [16, 512, 1024], P('expert', None, 'tensor'), may hold values from -8 to 8
- up_saved: bfloat16 [16, 512, 1024], P('expert', None, 'tensor'), may hold values from -6 to 6
- w_gate: bfloat16 [16, 4096, 1024], P('expert', None, 'tensor'), may hold values from -0.09375 to 0.09375
- w_up: bfloat16 [16, 4096, 1024], P('expert', None, 'tensor'), may hold values from -0.09375 to 0.09375
- w_down: bfloat16 [16, 1024, 4096], P('expert', 'tensor'), may hold values from -0.1875 to 0.1875
- out_proj: bfloat16 [4096, 4096], P('tensor', 'expert'), may hold values from -0.09375 to 0.09375
Outputs:
- resid_grad: bfloat16 [16, 32, 4096], P('expert', 'tensor')
- attn_grad: bfloat16 [16, 32, 4096], P('expert', None, 'tensor')
- down_grad: bfloat16 [16, 1024, 4096], P('expert', 'tensor')
Inputs may be any that keep to these rules, and one draw needn't show every extreme that they name: Each token names 8 different experts. Among the tokens of one group no expert is named by more than 32 routes, and in some group some expert is named by exactly 32.
All inputs are finite; a program needn't handle non-finite values.
Results may differ from a plain program's by a relative error of at most 0.015.
Values may be sent and summed in bfloat16 or wider, within the bound.
A program may use at most 128 MiB of HBM per device.

v0:
```python
import jax
import jax.numpy as jnp
from jax import lax
from jax.sharding import PartitionSpec as P


def slot_position(route_ids, slot_cap, expert_count):
    flat_ids = route_ids.reshape(-1)
    one_hot = (flat_ids[:, None] == jnp.arange(expert_count, dtype=jnp.int32)[None, :]).astype(
        jnp.int32
    )
    earlier = jnp.cumsum(one_hot, axis=0) - one_hot
    slot_rank = jnp.sum(earlier * one_hot, axis=1)
    return flat_ids * slot_cap + slot_rank


def weighted_rows(token_rows, slot_token, slot_weight):
    picked_rows = token_rows[slot_token]
    return (slot_weight[:, None] * picked_rows.astype(jnp.float32)).astype(jnp.bfloat16)


def per_device(
    out_grad,
    norm_input,
    norm_gain,
    routes,
    route_weight,
    gate_saved,
    up_saved,
    w_gate,
    w_up,
    w_down,
    out_proj,
):
    expert_count = lax.axis_size("expert")
    slot_cap = gate_saved.shape[1] // expert_count
    top_count = routes.shape[2]
    route_total = routes.shape[1] * top_count
    model_width = out_grad.shape[2]
    position = slot_position(routes[0], slot_cap, expert_count)
    source = (
        jnp.full((expert_count * slot_cap,), -1, jnp.int32)
        .at[position]
        .set(jnp.arange(route_total, dtype=jnp.int32))
    )
    filled = source >= 0
    safe_source = jnp.where(filled, source, 0)
    slot_weight = jnp.where(filled, route_weight[0].reshape(-1)[safe_source], jnp.float32(0.0))
    slot_token = safe_source // top_count
    group_grads = lax.all_gather(out_grad, "tensor", axis=1, tiled=True)
    scaled = weighted_rows(group_grads[0], slot_token, slot_weight)
    received = lax.all_to_all(
        scaled.reshape(expert_count, slot_cap, model_width),
        "expert",
        split_axis=0,
        concat_axis=0,
        tiled=True,
    )
    slot_grad = received.reshape(expert_count * slot_cap, model_width)
    contract_last = (((1,), (1,)), ((), ()))
    hid_grad = lax.dot_general(
        slot_grad, w_down[0], contract_last, preferred_element_type=jnp.float32
    )
    gate = gate_saved[0].astype(jnp.float32)
    upper = up_saved[0].astype(jnp.float32)
    sigmoid_gate = jax.nn.sigmoid(gate)
    activation = gate * sigmoid_gate
    gate_grad = (hid_grad * upper * sigmoid_gate * (1.0 + gate * (1.0 - sigmoid_gate))).astype(
        jnp.bfloat16
    )
    up_grad = (hid_grad * activation).astype(jnp.bfloat16)
    part_grad = lax.dot_general(
        gate_grad, w_gate[0], contract_last, preferred_element_type=jnp.float32
    )
    part_grad = part_grad + lax.dot_general(
        up_grad, w_up[0], contract_last, preferred_element_type=jnp.float32
    )
    part_grad = part_grad.astype(jnp.bfloat16)
    hidden = (activation * upper).astype(jnp.bfloat16)
    contract_first = (((0,), (0,)), ((), ()))
    block_sums = lax.psum_scatter(
        part_grad.astype(jnp.float32).astype(jnp.bfloat16),
        "tensor",
        scatter_dimension=1,
        tiled=True,
    ).astype(jnp.float32)
    feature_width = block_sums.shape[1]
    came_back = lax.all_to_all(
        block_sums.reshape(expert_count, slot_cap, feature_width).astype(jnp.bfloat16),
        "expert",
        split_axis=0,
        concat_axis=0,
        tiled=True,
    ).astype(jnp.float32)
    picked_part = came_back.reshape(expert_count * slot_cap, feature_width)[position]
    part_sum = jnp.sum(picked_part.reshape(-1, top_count, feature_width), axis=1)
    moe_grad = lax.all_to_all(
        part_sum.astype(jnp.bfloat16), "tensor", split_axis=0, concat_axis=1, tiled=True
    ).astype(part_sum.dtype)
    down_grad = lax.dot_general(
        hidden, slot_grad, contract_first, preferred_element_type=jnp.float32
    )
    down_grad = down_grad.astype(jnp.bfloat16)[None]
    resid_in = norm_input[0].astype(jnp.float32)
    inv_rms = lax.rsqrt(jnp.mean(resid_in * resid_in, axis=-1, keepdims=True) + 1e-06)
    scaled_grad = norm_gain * moe_grad
    projection = jnp.sum(scaled_grad * resid_in, axis=-1, keepdims=True)
    resid_grad = (
        out_grad[0].astype(jnp.float32)
        + inv_rms * scaled_grad
        - inv_rms * inv_rms * inv_rms / model_width * resid_in * projection
    )
    resid_grad = resid_grad.astype(jnp.bfloat16)[None]
    group_resid = lax.all_gather(resid_grad, "tensor", axis=1, tiled=True)
    group_rows = group_resid[0]
    attn_sum = lax.dot_general(
        group_rows,
        lax.all_gather(out_proj, "expert", axis=1, tiled=True),
        contract_last,
        preferred_element_type=jnp.float32,
    )
    attn_grad = attn_sum.astype(jnp.bfloat16)[None]
    return (resid_grad, attn_grad, down_grad)


def solution(mesh):
    placed = (
        P("expert", "tensor", None),
        P("expert", "tensor", None),
        P(),
        P("expert", None, None),
        P("expert", None, None),
        P("expert", None, "tensor"),
        P("expert", None, "tensor"),
        P("expert", None, "tensor"),
        P("expert", None, "tensor"),
        P("expert", "tensor", None),
        P("tensor", "expert"),
    )
    return jax.shard_map(
        per_device,
        mesh=mesh,
        in_specs=placed,
        out_specs=(
            P("expert", "tensor", None),
            P("expert", None, "tensor"),
            P("expert", "tensor", None),
        ),
        check_vma=False,
    )
```

profile of v0, /device:TPU:14, one launch (start us, length us, event | category | flops | bytes accessed | tf_op | source)
XLA Modules:
  0.0 344.6 jit_solution(199653472985301965)
XLA Ops:
  8.0 0.8 copy.20
  9.0 0.7 broadcast_multiply_fusion
  10.8 1.4 scatter_custom_fusion
  12.2 0.8 copy.23
  13.1 3.5 %gather_fusion = f32[512]{0:T(512)S(1)} fusion(f32[256]{0:T(256)S(1)} %reshape_squeeze.4, s32[1024]{0:T(1024)S(1)} %pad_clamp_fusion.2), kind=kCustom, calls=%fused_computation | custom fusion | bytes 6144 | tf_op jit(solution)/shard_map/gather | solution.py:48
  16.7 6.1 %all_gather.9 = bf16[1,32,4096]{2,1,0:T(8,128)(2,1)S(1)} all-gather(bf16[1,16,4096]{2,1,0:T(8,128)(2,1)} %param.11), channel_id=1, replica_groups=mesh['tensor'=2,'expert'=16] {'tensor'}, dimensions={1}, use_global_device_ids=true | all-gather | bytes 393216 | tf_op jit(solution)/shard_map/all_gather | solution.py:50
  22.8 4.4 %gather_fusion.1 = bf16[512,4096]{1,0:T(8,128)(2,1)} fusion(bf16[32,4096]{1,0:T(8,128)(2,1)S(1)} %bitcast.101, s32[1024]{0:T(1024)S(1)} %pad_clamp_fusion.1), kind=kCustom, calls=%fused_computation.1 | custom fusion | bytes 8390656 | tf_op jit(solution)/shard_map/gather | solution.py:18
  27.2 3.7 %fusion = bf16[16,32,4096]{2,1,0:T(8,128)(2,1)S(1)} fusion(bf16[16,32,4096]{2,1,0:T(8,128)(2,1)} %bitcast.102, f32[16,32]{1,0:T(8,128)S(1)} %mul.144), kind=kLoop, calls=%fused_computation.5 | loop fusion | flops 6291456 | bytes 8390656 | tf_op jit(solution)/shard_map/convert_element_type | solution.py:19
  30.9 98.2 %all_to_all.20 = bf16[16,32,4096]{2,1,0:T(8,128)(2,1)S(1)} all-to-all(bf16[16,32,4096]{2,1,0:T(8,128)(2,1)S(1)} %fusion), channel_id=1, replica_groups=mesh['tensor'=2,'expert'=16] {'expert'}, dimensions={0} | all-to-all | bytes 8388608 | tf_op jit(solution)/shard_map/all_to_all | solution.py:52
  129.1 1.9 copy-done
  131.1 2.4 fusion.5
  133.5 2.6 fusion.3
  136.1 4.5 %add_convert_fusion = bf16[512,4096]{1,0:T(8,128)(2,1)} fusion(f32[512,4096]{1,0:T(8,128)S(1)} %fusion.3, bf16[1,4096,512]{2,1,0:T(8,128)(2,1)S(1)} %copy-done.3, f32[512,512]{1,0:T(8,128)S(1)} %fusion.5, bf16[1,512,512]{2,1,0:T(8,128)(2,1)S(1)} %copy-done.1), kind=kOutput, calls=%fused_computation.6 | convolution fusion | flops 2153512960 | bytes 18350080 | tf_op jit(solution)/shard_map/dot_general | solution.py:75
  141.2 53.4 %reduce-scatter.2.cloned.1.call-done = bf16[512,2048]{1,0:T(8,128)(2,1)} async-done(((bf16[512,4096]{1,0:T(8,128)(2,1)}), bf16[512,2048]{1,0:T(8,128)(2,1)}) %reduce-scatter.2.cloned.1.call-update) | async-done | bytes 2097168 | tf_op jit(solution)/shard_map/reduce_scatter | solution.py:81
  194.6 6.1 %all-to-all-start.1 = ((bf16[16,32,2048]{2,1,0:T(8,128)(2,1)}), bf16[16,32,2048]{2,1,0:T(8,128)(2,1)S(1)}, u32[]{:S(2)}, u32[]{:S(2)}) async-start(bf16[16,32,2048]{2,1,0:T(8,128)(2,1)} %bitcast.105), calls=%async_computation.2 | async-start | bytes 4194304 | tf_op jit(solution)/shard_map/all_to_all | solution.py:88
  201.6 1.2 pad_clamp_fusion
  203.5 96.2 %all-to-all-done.1 = bf16[16,32,2048]{2,1,0:T(8,128)(2,1)S(1)} async-done(((bf16[16,32,2048]{2,1,0:T(8,128)(2,1)}), bf16[16,32,2048]{2,1,0:T(8,128)(2,1)S(1)}, u32[]{:S(2)}, u32[]{:S(2)}) %all-to-all-start.1) | async-done | bytes 2097184 | tf_op jit(solution)/shard_map/all_to_all | solution.py:88
  299.7 2.7 bitcast_convert_fusion
  302.3 4.7 %gather_fusion.2 = f32[256,2048]{1,0:T(8,128)S(1)} fusion(f32[512,2048]{1,0:T(8,128)} %bitcast_convert_fusion, s32[1024]{0:T(1024)} %pad_clamp_fusion), kind=kCustom, calls=%fused_computation.2 | custom fusion | bytes 4195328 | tf_op jit(solution)/shard_map/gather | solution.py:95
  307.1 1.2 bitcast_reduce_fusion
  308.2 3.9 %all-to-all-start.2 = ((bf16[2,16,2048]{2,1,0:T(8,128)(2,1)}), bf16[2,16,2048]{2,1,0:T(8,128)(2,1)S(1)}, u32[]{:S(2)}, u32[]{:S(2)}) async-start(bf16[2,16,2048]{2,1,0:T(8,128)(2,1)} %bitcast.106), calls=%async_computation.3 | async-start | bytes 262144 | tf_op jit(solution)/shard_map/all_to_all | solution.py:97
  312.2 6.9 %fusion.1 = bf16[1,512,4096]{2,1,0:T(8,128)(2,1)} fusion(bf16[512,4096]{1,0:T(8,128)(2,1)} %bitcast.104, bf16[1,512,512]{2,1,0:T(8,128)(2,1)S(1)} %copy-done.4, bf16[1,512,512]{2,1,0:T(8,128)(2,1)S(1)} %copy-done.1), kind=kOutput, calls=%fused_computation.8 | convolution fusion | flops 2151677952 | bytes 9437184 | tf_op jit(solution)/shard_map/dot_general | solution.py:100
  319.9 5.8 %all_gather.10 = bf16[1,32,4096]{2,1,0:T(8,128)(2,1)S(1)} all-gather(bf16[1,16,4096]{2,1,0:T(8,128)(2,1)S(1)} %subtract_convert_fusion), channel_id=1, replica_groups=mesh['tensor'=2,'expert'=16] {'tensor'}, dimensions={1}, use_global_device_ids=true | all-gather | bytes 393216 | tf_op jit(solution)/shard_map/all_gather | solution.py:114
  325.7 11.5 %fusion.7 = bf16[1,32,2048]{2,1,0:T(8,128)(2,1)} fusion(bf16[2048,4096]{1,0:T(8,128)(2,1)} %all-gather.2.cloned.1.call-done, bf16[1,32,4096]{2,1,0:T(8,128)(2,1)S(1)} %all_gather.10), kind=kOutput, calls=%fused_computation.15 | convolution fusion | flops 536936448 | bytes 17170432 | tf_op jit(solution)/shard_map/dot_general | solution.py:116
  (60 shorter events, 4.6 us)
Async XLA Ops:
  8.0 186.6 %reduce-scatter.2.cloned.1.call-start = ((), (), s32[]{:S(2)}) async-start(), calls=%async_computation.4 | async-start | bytes 6291456 | tf_op jit(solution)/shard_map/reduce_scatter | solution.py:81
  10.8 1.5 copy-start.10
  30.9 100.2 %copy-start.13 = (bf16[1,512,4096]{2,1,0:T(8,128)(2,1)S(1)}, bf16[1,512,4096]{2,1,0:T(8,128)(2,1)}, u32[]{:S(2)}) copy-start(bf16[1,512,4096]{2,1,0:T(8,128)(2,1)} %param.20) | copy-start | bytes 12582916
  129.1 1.9 copy-start
  131.1 2.4 copy-start.1
  131.1 2.4 copy-start.2
  131.1 2.5 copy-start.4
  133.5 2.6 copy-start.3
  140.6 60.1 %copy-start.5 = (bf16[1,16,4096]{2,1,0:T(8,128)(2,1)S(1)}, bf16[1,16,4096]{2,1,0:T(8,128)(2,1)}, u32[]{:S(2)}) copy-start(bf16[1,16,4096]{2,1,0:T(8,128)(2,1)} %param.12) | copy-start | bytes 393220
  140.6 60.4 %copy-start.8 = (f32[4096]{0:T(1024)S(1)}, f32[4096]{0:T(1024)}, u32[]{:S(2)}) copy-start(f32[4096]{0:T(1024)} %param.13) | copy-start | bytes 49156
  140.6 185.1 %all-gather.2.cloned.1.call-start = ((), (), s32[]{:S(2)}) async-start(), calls=%async_computation.5 | async-start | bytes 17825792 | tf_op jit(solution)/shard_map/all_gather | solution.py:118
  194.6 105.1 %all-to-all-start.1 = ((bf16[16,32,2048]{2,1,0:T(8,128)(2,1)}), bf16[16,32,2048]{2,1,0:T(8,128)(2,1)S(1)}, u32[]{:S(2)}, u32[]{:S(2)}) async-start(bf16[16,32,2048]{2,1,0:T(8,128)(2,1)} %bitcast.105), calls=%async_computation.2 | async-start | bytes 4194304 | tf_op jit(solution)/shard_map/all_to_all | solution.py:88
  308.2 10.8 %all-to-all-start.2 = ((bf16[2,16,2048]{2,1,0:T(8,128)(2,1)}), bf16[2,16,2048]{2,1,0:T(8,128)(2,1)S(1)}, u32[]{:S(2)}, u32[]{:S(2)}) async-start(bf16[2,16,2048]{2,1,0:T(8,128)(2,1)} %bitcast.106), calls=%async_computation.3 | async-start | bytes 262144 | tf_op jit(solution)/shard_map/all_to_all | solution.py:97
  312.1 7.4 %copy-start.9 = (f32[2,2048]{1,0:T(2,128)S(1)}, f32[2,2048]{1,0:T(2,128)}, u32[]{:S(2)}) copy-start(f32[2,2048]{1,0:T(2,128)} %mul.159) | copy-start | bytes 49156
  312.1 7.6 %copy-start.6 = (bf16[1,16,4096]{2,1,0:T(8,128)(2,1)S(1)}, bf16[1,16,4096]{2,1,0:T(8,128)(2,1)}, u32[]{:S(2)}) copy-start(bf16[1,16,4096]{2,1,0:T(8,128)(2,1)} %param.11) | copy-start | bytes 393220
  312.1 7.6 %copy-start.11 = (f32[16]{0:T(128)S(1)}, f32[16]{0:T(128)}, u32[]{:S(2)}) copy-start(f32[16]{0:T(128)} %get-tuple-element.5) | copy-start | bytes 196
  312.2 7.6 %copy-start.12 = (f32[16]{0:T(128)S(1)}, f32[16]{0:T(128)}, u32[]{:S(2)}) copy-start(f32[16]{0:T(128)} %get-tuple-element.6) | copy-start | bytes 196
  319.9 17.2 %copy-start.7 = (bf16[1,16,4096]{2,1,0:T(8,128)(2,1)}, bf16[1,16,4096]{2,1,0:T(8,128)(2,1)S(1)}, u32[]{:S(2)}) copy-start(bf16[1,16,4096]{2,1,0:T(8,128)(2,1)S(1)} %subtract_convert_fusion) | copy-start | bytes 393220
Sparse Core Ops, SparseCore 0:
  140.7 53.8 reduce-scatter.1
Sparse Core Ops, SparseCore 1:
  143.2 172.4 all-gather.1
where the time goes:
time: 345 us
  waiting for transfers between devices  150 us (43%)
  blocking collectives  110 us (32%)
  matrix products  27.7 us (8%)
  local copies, waits for them, and re-layouts  19.6 us (6%)
  between operations  15.7 us (5%)
  other arithmetic  11.3 us (3%)
  starting transfers between devices  10.1 us (3%)
    all_to_all x1, blocking collectives, per_device(): lax.all_to_all(scaled.reshape(expert_count, slot_cap, model_width), 'expe...  98.2 us
    all_to_all x1, waiting for transfers between devices, per_device(): lax.all_to_all(block_sums.reshape(expert_count, slot_cap, feature_width)....  96.2 us
    reduce_scatter x1, waiting for transfers between devices, per_device(): lax.psum_scatter(part_grad.astype(jnp.float32).astype(jnp.bfloat16), 'ten...  53.4 us
    dot_general x1, matrix products, per_device(): lax.dot_general(group_rows, lax.all_gather(out_proj, 'expert', axis=1, ti...  11.5 us
  transfers between devices with their start and end apart: 4, of which 2 were waited for; matrix products, arithmetic and copies ran while one was open for 6% of the time, Pallas kernels for 0%

commit v1 on v0

--- a/solution.py
+++ b/solution.py
@@ -19,7 +19,7 @@
     return (slot_weight[:, None] * picked_rows.astype(jnp.float32)).astype(jnp.bfloat16)
 
 
-def per_device(
+def per_device_slots(
     out_grad,
     norm_input,
     norm_gain,
@@ -123,6 +123,114 @@
     return (resid_grad, attn_grad, down_grad)
 
 
+def per_device_tokens(
+    out_grad,
+    norm_input,
+    norm_gain,
+    routes,
+    route_weight,
+    gate_saved,
+    up_saved,
+    w_gate,
+    w_up,
+    w_down,
+    out_proj,
+):
+    everyone = ("expert", "tensor")
+    expert_count = lax.axis_size("expert")
+    expert = lax.axis_index("expert")
+    slot_total = gate_saved.shape[1]
+    slot_cap = slot_total // expert_count
+    group_tokens = routes.shape[1]
+    model_width = out_grad.shape[2]
+    token_total = expert_count * group_tokens
+    contract_last = (((1,), (1,)), ((), ()))
+    contract_first = (((0,), (0,)), ((), ()))
+
+    dense = jnp.sum(
+        jnp.where(
+            routes[0][:, :, None] == jnp.arange(expert_count, dtype=jnp.int32)[None, None, :],
+            route_weight[0][:, :, None],
+            0.0,
+        ),
+        axis=1,
+    )
+    all_dense = lax.all_gather(dense, "expert", axis=0, tiled=False)
+    weight = lax.dynamic_index_in_dim(all_dense, expert, axis=2, keepdims=False)
+    named = weight > 0.0
+    before = jnp.tril(jnp.ones((group_tokens, group_tokens), jnp.float32), -1)
+    rank = jnp.einsum("gt,ut->gu", named.astype(jnp.float32), before).astype(jnp.int32)
+    slot = jnp.arange(expert_count, dtype=jnp.int32)[:, None] * slot_cap + rank
+    slot = jnp.where(named, slot, -1).reshape(token_total, 1)
+    pick = (slot == jnp.arange(slot_total, dtype=jnp.int32)[None, :]).astype(jnp.bfloat16)
+    gate = lax.dot_general(
+        pick, gate_saved[0], (((1,), (0,)), ((), ())), preferred_element_type=jnp.float32
+    )
+    upper = lax.dot_general(
+        pick, up_saved[0], (((1,), (0,)), ((), ())), preferred_element_type=jnp.float32
+    )
+    sigmoid_gate = jax.nn.sigmoid(gate)
+    activation = gate * sigmoid_gate
+    hidden = (activation * upper).astype(jnp.bfloat16)
+
+    all_grads = lax.all_gather(out_grad[0], everyone, axis=0, tiled=True)
+    token_grad = (weight.reshape(token_total, 1) * all_grads.astype(jnp.float32)).astype(
+        jnp.bfloat16
+    )
+    hid_grad = lax.dot_general(
+        token_grad, w_down[0], contract_last, preferred_element_type=jnp.float32
+    )
+    gate_grad = (hid_grad * upper * sigmoid_gate * (1.0 + gate * (1.0 - sigmoid_gate))).astype(
+        jnp.bfloat16
+    )
+    up_grad = (hid_grad * activation).astype(jnp.bfloat16)
+    part_grad = lax.dot_general(
+        gate_grad, w_gate[0], contract_last, preferred_element_type=jnp.float32
+    )
+    part_grad = part_grad + lax.dot_general(
+        up_grad, w_up[0], contract_last, preferred_element_type=jnp.float32
+    )
+    part_grad = part_grad.astype(jnp.bfloat16)
+    moe_grad = lax.psum_scatter(
+        part_grad, everyone, scatter_dimension=0, tiled=True
+    ).astype(jnp.float32)
+    down_grad = lax.dot_general(
+        hidden, token_grad, contract_first, preferred_element_type=jnp.float32
+    )
+    down_grad = down_grad.astype(jnp.bfloat16)[None]
+    resid_in = norm_input[0].astype(jnp.float32)
+    inv_rms = lax.rsqrt(jnp.mean(resid_in * resid_in, axis=-1, keepdims=True) + 1e-06)
+    scaled_grad = norm_gain * moe_grad
+    projection = jnp.sum(scaled_grad * resid_in, axis=-1, keepdims=True)
+    resid_grad = (
+        out_grad[0].astype(jnp.float32)
+        + inv_rms * scaled_grad
+        - inv_rms * inv_rms * inv_rms / model_width * resid_in * projection
+    )
+    resid_grad = resid_grad.astype(jnp.bfloat16)
+    own_rows = resid_grad.shape[0]
+    columns = lax.all_to_all(
+        resid_grad.reshape(own_rows, expert_count, -1),
+        "expert",
+        split_axis=1,
+        concat_axis=0,
+        tiled=True,
+    ).reshape(expert_count, own_rows, -1)
+    columns = lax.all_gather(columns, "tensor", axis=1, tiled=True).reshape(token_total, -1)
+    attn_part = lax.dot_general(
+        columns, out_proj, contract_last, preferred_element_type=jnp.float32
+    ).astype(jnp.bfloat16)
+    attn_grad = lax.psum_scatter(attn_part, "expert", scatter_dimension=0, tiled=True)
+    return (resid_grad[None], attn_grad[None], down_grad)
+
+
+def per_device(*args):
+    token_total = lax.axis_size("expert") * args[3].shape[1]
+    if token_total <= args[5].shape[1]:
+        return per_device_tokens(*args)
+    return per_device_slots(*args)
+
+
 def solution(mesh):
     placed = (
         P("expert", "tensor", None),

time: 345 us -> 319 us (0.925)
  the two profiles are of different devices: /device:TPU:14 before, /device:TPU:0 now
where the time goes in v1:
time: 319 us; the launch traced here: 318 us
  waiting for transfers between devices  235 us (74%)
  blocking collectives  39.6 us (12%)
  matrix products  26.1 us (8%)
  between operations  13.9 us (4%)
    reduce_scatter x1, waiting for transfers between devices, per_device_tokens(): lax.psum_scatter(part_grad, everyone, scatter_dimension=0, tiled=True)  143 us
    reduce_scatter x1, waiting for transfers between devices, per_device_tokens(): lax.psum_scatter(attn_part, 'expert', scatter_dimension=0, tiled=True)  52.5 us
    all_gather x1, waiting for transfers between devices, per_device_tokens(): all_grads = lax.all_gather(out_grad[0], everyone, axis=0, tiled=True)  39 us
    all_gather x1, blocking collectives, per_device_tokens(): all_dense = lax.all_gather(dense, 'expert', axis=0, tiled=False)  23.5 us
    all_to_all x1, blocking collectives, per_device_tokens(): lax.all_to_all(resid_grad.reshape(own_rows, expert_count, -1), 'expert',...  10.5 us
    dot_general x1, matrix products, per_device_tokens(): lax.dot_general(hidden, token_grad, contract_first, preferred_element_typ...  6.79 us
  transfers between devices with their start and end apart: 3, of which 3 were waited for; matrix products, arithmetic and copies ran while one was open for 4% of the time, Pallas kernels for 0%

profile of v1, /device:TPU:0, one launch (start us, length us, event | category | flops | bytes accessed | tf_op | source)
XLA Modules:
  0.0 318.3 jit_solution(6439463695742115034)
XLA Ops:
  7.2 0.0 all-gather.6.cloned.1.call-start
  7.2 0.7 all-gather.6.cloned.1.call-update
  7.9 0.0 reduce-scatter.3.cloned.1.call-start
  8.0 0.7 select_reduce_fusion
  8.7 23.5 %all-gather.3 = f32[16,32,16]{1,2,0:T(8,128)S(1)} all-gather(f32[1,32,16]{1,2,0:T(8,128)S(1)} %bitcast.56), channel_id=2, replica_groups=mesh['tensor'=2,'expert'=16] {'expert'}, dimensions={0}, use_global_device_ids=true | all-gather | bytes 34816 | tf_op jit(solution)/shard_map/all_gather | solution.py:158
  32.2 0.1 mul.96
  32.3 0.2 fusion.10
  32.5 0.1 eq.34
  32.6 1.5 fusion.12
  34.1 2.5 fusion.13
  36.7 39.0 %all-gather.6.cloned.1.call-done = bf16[1,512,4096]{2,1,0:T(8,128)(2,1)} async-done(((bf16[1,16,4096]{2,1,0:T(8,128)(2,1)}), bf16[1,512,4096]{2,1,0:T(8,128)(2,1)}) %all-gather.6.cloned.1.call-update) | async-done | bytes 4194320 | tf_op jit(solution)/shard_map/all_gather | solution.py:176
  75.7 6.0 %fusion.5 = f32[512,512]{1,0:T(8,128)S(1)} fusion(bf16[1,512,4096]{2,1,0:T(8,128)(2,1)} %param.20, bf16[1,512,4096]{2,1,0:T(8,128)(2,1)} %all-gather.6.cloned.1.call-done, f32[512]{0:T(512)S(1)} %mul.96), kind=kOutput, calls=%fused_computation.8 | convolution fusion | flops 2153775104 | bytes 9439232 | tf_op jit(solution)/shard_map/dot_general | solution.py:180
  81.7 2.6 fusion.3
  84.3 4.4 %add_convert_fusion = bf16[512,4096]{1,0:T(8,128)(2,1)} fusion(f32[512,4096]{1,0:T(8,128)S(1)} %fusion.3, bf16[1,4096,512]{2,1,0:T(8,128)(2,1)S(1)} %copy-done.2, f32[512,512]{1,0:T(8,128)S(1)} %fusion.5, f32[512,512]{1,0:T(8,128)S(1)} %fusion.12), kind=kOutput, calls=%fused_computation.2 | convolution fusion | flops 2153250816 | bytes 18874368 | tf_op jit(solution)/shard_map/dot_general | solution.py:190
  88.8 0.0 reduce-scatter.5.cloned.1.call-start
  88.8 143.2 %reduce-scatter.3.cloned.1.call-done = bf16[16,4096]{1,0:T(8,128)(2,1)} async-done(((bf16[512,4096]{1,0:T(8,128)(2,1)}), bf16[16,4096]{1,0:T(8,128)(2,1)}) %reduce-scatter.3.cloned.1.call-update) | async-done | bytes 131088 | tf_op jit(solution)/shard_map/reduce_scatter | solution.py:194
  232.1 1.1 fusion.19
  233.2 1.0 fusion.22
  234.2 10.5 %all_to_all.15 = bf16[16,16,256]{2,0,1:T(8,128)(2,1)S(1)} all-to-all(bf16[16,16,256]{2,0,1:T(8,128)(2,1)S(1)} %bitcast.55), channel_id=1, replica_groups=mesh['tensor'=2,'expert'=16] {'expert'}, dimensions={1} | all-to-all | bytes 262144 | tf_op jit(solution)/shard_map/all_to_all | solution.py:212
  244.7 5.6 %all-gather.2 = bf16[16,32,1,256]{3,1,0,2:T(8,128)(2,1)S(1)} all-gather(bf16[16,16,1,256]{3,1,0,2:T(8,128)(2,1)S(1)} %bitcast.54), channel_id=4, replica_groups=mesh['tensor'=2,'expert'=16] {'tensor'}, dimensions={1}, use_global_device_ids=true | all-gather | bytes 393216 | tf_op jit(solution)/shard_map/all_gather | solution.py:219
  250.4 2.1 convolution_convert_fusion.1
  252.4 0.0 reduce-scatter.5.cloned.1.call-update
  252.5 6.8 %fusion.1 = bf16[1,512,4096]{2,1,0:T(8,128)(2,1)} fusion(bf16[1,512,4096]{2,1,0:T(8,128)(2,1)} %all-gather.6.cloned.1.call-done, f32[512]{0:T(512)} %copy-done.9, f32[512,512]{1,0:T(8,128)S(1)} %copy-done.4, f32[512,512]{1,0:T(8,128)S(1)} %fusion.12), kind=kOutput, calls=%fused_computation.4 | convolution fusion | flops 2157445120 | bytes 10487808 | tf_op jit(solution)/shard_map/dot_general | solution.py:197
  259.2 52.5 %reduce-scatter.5.cloned.1.call-done = bf16[32,2048]{1,0:T(8,128)(2,1)} async-done(((bf16[512,2048]{1,0:T(8,128)(2,1)}), bf16[32,2048]{1,0:T(8,128)(2,1)}) %reduce-scatter.5.cloned.1.call-update) | async-done | bytes 131088 | tf_op jit(solution)/shard_map/reduce_scatter | solution.py:223
  (26 shorter events, 0.1 us)
Async XLA Ops:
  7.2 243.2 %copy-start = (bf16[2048,256]{1,0:T(8,128)(2,1)S(1)}, bf16[2048,256]{1,0:T(8,128)(2,1)}, u32[]{:S(2)}) copy-start(bf16[2048,256]{1,0:T(8,128)(2,1)} %param.21) | copy-start | bytes 3145732
  7.2 68.5 %all-gather.6.cloned.1.call-start = ((), (), s32[]{:S(2)}) async-start(), calls=%async_computation.5 | async-start | bytes 4325376 | tf_op jit(solution)/shard_map/all_gather | solution.py:176
  7.9 224.1 %reduce-scatter.3.cloned.1.call-start = ((), (), s32[]{:S(2)}) async-start(), calls=%async_computation.3 | async-start | bytes 4325376 | tf_op jit(solution)/shard_map/reduce_scatter | solution.py:194
  32.3 52.0 %copy-start.9 = (f32[512]{0:T(512)}, f32[512]{0:T(512)S(1)}, u32[]{:S(2)}) copy-start(f32[512]{0:T(512)S(1)} %mul.96) | copy-start | bytes 6148
  75.6 6.0 %copy-start.1 = (bf16[1,4096,512]{2,1,0:T(8,128)(2,1)S(1)}, bf16[1,4096,512]{2,1,0:T(8,128)(2,1)}, u32[]{:S(2)}) copy-start(bf16[1,4096,512]{2,1,0:T(8,128)(2,1)} %param.18) | copy-start | bytes 12582916
  75.6 6.0 %copy-start.3 = (f32[512,512]{1,0:T(8,128)S(1)}, f32[512,512]{1,0:T(8,128)}, u32[]{:S(2)}) copy-start(f32[512,512]{1,0:T(8,128)} %fusion.13) | copy-start | bytes 3145732
  81.6 2.7 copy-start.2
  88.7 143.3 %copy-start.6 = (bf16[1,16,4096]{2,1,0:T(8,128)(2,1)S(1)}, bf16[1,16,4096]{2,1,0:T(8,128)(2,1)}, u32[]{:S(2)}) copy-start(bf16[1,16,4096]{2,1,0:T(8,128)(2,1)} %param.12) | copy-start | bytes 393220
  88.7 143.3 %copy-start.8 = (f32[4096]{0:T(1024)S(1)}, f32[4096]{0:T(1024)}, u32[]{:S(2)}) copy-start(f32[4096]{0:T(1024)} %param.13) | copy-start | bytes 49156
  88.7 144.4 %copy-start.5 = (bf16[1,16,4096]{2,1,0:T(8,128)(2,1)S(1)}, bf16[1,16,4096]{2,1,0:T(8,128)(2,1)}, u32[]{:S(2)}) copy-start(bf16[1,16,4096]{2,1,0:T(8,128)(2,1)} %param.11) | copy-start | bytes 393220
  88.8 163.7 %copy-start.4 = (f32[512,512]{1,0:T(8,128)S(1)}, f32[512,512]{1,0:T(8,128)}, u32[]{:S(2)}) copy-start(f32[512,512]{1,0:T(8,128)} %fusion.13) | copy-start | bytes 3145732
  88.8 223.0 %reduce-scatter.5.cloned.1.call-start = ((), (), s32[]{:S(2)}) async-start(), calls=%async_computation.4 | async-start | bytes 2228224 | tf_op jit(solution)/shard_map/reduce_scatter | solution.py:223
  234.2 25.0 %copy-start.7 = (bf16[16,4096]{1,0:T(8,128)(2,1)}, bf16[16,4096]{1,0:T(8,128)(2,1)S(1)}, u32[]{:S(2)}) copy-start(bf16[16,4096]{1,0:T(8,128)(2,1)S(1)} %fusion.22) | copy-start | bytes 393220
Sparse Core Ops, SparseCore 0:
  11.0 64.6 all-gather.5
  88.9 143.1 reduce-scatter.2
  252.6 59.1 reduce-scatter.4

commit v2 on v1

--- a/solution.py
+++ b/solution.py
@@ -1,6 +1,9 @@
+import functools
 import jax
 import jax.numpy as jnp
 from jax import lax
+from jax.experimental import pallas as pl
+from jax.experimental.pallas import tpu as pltpu
 from jax.sharding import PartitionSpec as P
 
 
@@ -123,6 +126,443 @@
     return (resid_grad, attn_grad, down_grad)
 
 
+MESH_ID = pl.DeviceIdType.MESH
+ROUTE_LANES = 128
+GATHER_ORDERS = (("z", "y", "x"), ("z", "x", "y"), ("x", "z", "y"), ("y", "z", "x"))
+VMEM_SPEC = pl.BlockSpec(memory_space=pltpu.VMEM)
+
+
+def place():
+    expert = lax.axis_index("expert")
+    return {
+        "z": expert // 4,
+        "y": lax.rem(expert // 2, 2),
+        "c": lax.rem(expert, 2),
+        "x": lax.axis_index("tensor"),
+    }
+
+
+def device_at(at):
+    return {"expert": (at["z"] * 2 + at["y"]) * 2 + at["c"], "tensor": at["x"]}
+
+
+def moved(at, axis, step, sizes):
+    return {**at, axis: lax.rem(at[axis] + step, sizes[axis])}
+
+
+def greet(at, sizes, axes):
+    barrier = pltpu.get_barrier_semaphore()
+    count = 0
+    for axis in axes:
+        for step in range(1, sizes[axis]):
+            pl.semaphore_signal(
+                barrier,
+                inc=1,
+                device_id=device_at(moved(at, axis, step, sizes)),
+                device_id_type=MESH_ID,
+            )
+            count += 1
+    pl.semaphore_wait(barrier, count)
+
+
+def column_chunks(width, count):
+    tiles = width // 128
+    edges = [tiles * i // count * 128 for i in range(count + 1)]
+    return [(edges[i], edges[i + 1] - edges[i]) for i in range(count)]
+
+
+def gather_kernel(sizes, x_ref, out_ref, own_sem, send_sem, recv_sem):
+    at = place()
+    chunks = column_chunks(x_ref.shape[1], len(GATHER_ORDERS))
+    own = pltpu.make_async_copy(
+        x_ref, out_ref.at[at["z"], at["y"], at["c"], at["x"]], own_sem
+    )
+    own.start()
+    greet(at, sizes, "zyxc")
+    own.wait()
+
+    def stage(chunk, number, axis, done):
+        start, width = chunks[chunk]
+        index = tuple(
+            slice(None) if name in done else at[name] for name in "zycx"
+        ) + (slice(None), pl.ds(start, width))
+        copies = []
+        for step in range(1, sizes[axis]):
+            copy = pltpu.make_async_remote_copy(
+                src_ref=out_ref.at[index],
+                dst_ref=out_ref.at[index],
+                send_sem=send_sem.at[chunk, number, step - 1],
+                recv_sem=recv_sem.at[chunk, number, step - 1],
+                device_id=device_at(moved(at, axis, step, sizes)),
+                device_id_type=MESH_ID,
+            )
+            copy.start()
+            copies.append(copy)
+        return copies
+
+    pending = {}
+    everything = []
+    for number in range(4):
+        for chunk, order in enumerate(GATHER_ORDERS):
+            full = order + ("c",)
+            for copy in pending.get(chunk, ()):
+                copy.wait_recv()
+            pending[chunk] = stage(chunk, number, full[number], full[:number])
+            everything += pending[chunk]
+    for chunk in range(len(GATHER_ORDERS)):
+        for copy in pending[chunk]:
+            copy.wait_recv()
+    for copy in everything:
+        copy.wait_send()
+
+
+def gather_all(rows, sizes):
+    shape = (sizes["z"], sizes["y"], sizes["c"], sizes["x"]) + rows.shape
+    most = max(sizes.values()) - 1
+    count = len(GATHER_ORDERS)
+    return pl.pallas_call(
+        functools.partial(gather_kernel, sizes),
+        out_shape=jax.ShapeDtypeStruct(shape, rows.dtype),
+        in_specs=[VMEM_SPEC],
+        out_specs=VMEM_SPEC,
+        scratch_shapes=[
+            pltpu.SemaphoreType.DMA,
+            pltpu.SemaphoreType.DMA((count, 4, most)),
+            pltpu.SemaphoreType.DMA((count, 4, most)),
+        ],
+        compiler_params=pltpu.CompilerParams(collective_id=0, has_side_effects=True),
+    )(rows)
+
+
+def added(first, second):
+    return (first.astype(jnp.float32) + second.astype(jnp.float32)).astype(jnp.bfloat16)
+
+
+def scatter_kernel(
+    sizes,
+    part_ref,
+    out_grad_ref,
+    norm_input_ref,
+    norm_gain_ref,
+    resid_ref,
+    acc_ref,
+    from_core,
+    from_x,
+    from_y,
+    from_z,
+    moe_ref,
+    send_sem,
+    recv_sem,
+):
+    at = place()
+    width_all = part_ref.shape[-1]
+    chunks = column_chunks(width_all, len(GATHER_ORDERS))
+    landing = {"x": from_x, "y": from_y, "z": from_z}
+    greet(at, sizes, "zyxc")
+    everything = []
+
+    def send(source, target, axis, step, chunk, number):
+        copy = pltpu.make_async_remote_copy(
+            src_ref=source,
+            dst_ref=target,
+            send_sem=send_sem.at[chunk, number, step - 1],
+            recv_sem=recv_sem.at[chunk, number, step - 1],
+            device_id=device_at(moved(at, axis, step, sizes)),
+            device_id_type=MESH_ID,
+        )
+        copy.start()
+        everything.append(copy)
+        return copy
+
+    pending = {}
+    for chunk, (start, width) in enumerate(chunks):
+        cols = pl.ds(start, width)
+        pending[chunk] = [
+            send(
+                part_ref.at[:, :, 1 - at["c"], :, :, cols],
+                from_core.at[:, :, :, :, cols],
+                "c",
+                1,
+                chunk,
+                0,
+            )
+        ]
+    for number in range(1, 5):
+        for chunk, (start, width) in enumerate(chunks):
+            cols = pl.ds(start, width)
+            order = GATHER_ORDERS[chunk][::-1]
+            for copy in pending[chunk]:
+                copy.wait_recv()
+            if number == 1:
+                for z in range(sizes["z"]):
+                    acc_ref[z, :, :, :, cols] = added(
+                        part_ref[z, :, at["c"], :, :, cols], from_core[z, :, :, :, cols]
+                    )
+            else:
+                axis, left = order[number - 2], order[number - 1:]
+                where = tuple(slice(None) if n in left else at[n] for n in "zyx")
+                total = acc_ref[where + (slice(None), cols)].astype(jnp.float32)
+                for step in range(1, sizes[axis]):
+                    index = (step - 1,) + tuple(
+                        slice(None) if n in left else 0 for n in "zyx"
+                    )
+                    total = total + landing[axis][index + (slice(None), cols)].astype(
+                        jnp.float32
+                    )
+                if number == 4:
+                    moe_ref[:, cols] = total
+                else:
+                    acc_ref[where + (slice(None), cols)] = total.astype(jnp.bfloat16)
+            if number < 4:
+                axis, left = order[number - 1], order[number:]
+                pending[chunk] = []
+                for step in range(1, sizes[axis]):
+                    to = moved(at, axis, step, sizes)
+                    source = tuple(slice(None) if n in left else to[n] for n in "zyx")
+                    target = (step - 1,) + tuple(
+                        slice(None) if n in left else 0 for n in "zyx"
+                    )
+                    pending[chunk].append(
+                        send(
+                            acc_ref.at[source + (slice(None), cols)],
+                            landing[axis].at[target + (slice(None), cols)],
+                            axis,
+                            step,
+                            chunk,
+                            number,
+                        )
+                    )
+    resid_in = norm_input_ref[...].astype(jnp.float32)
+    inv_rms = lax.rsqrt(jnp.mean(resid_in * resid_in, axis=-1, keepdims=True) + 1e-06)
+    scaled_grad = norm_gain_ref[...] * moe_ref[...]
+    projection = jnp.sum(scaled_grad * resid_in, axis=-1, keepdims=True)
+    resid_grad = (
+        out_grad_ref[...].astype(jnp.float32)
+        + inv_rms * scaled_grad
+        - inv_rms * inv_rms * inv_rms / width_all * resid_in * projection
+    )
+    resid_ref[...] = resid_grad.astype(jnp.bfloat16)
+    for copy in everything:
+        copy.wait_send()
+
+
+def scatter_and_norm(part, out_grad, norm_input, norm_gain, sizes):
+    rows, width = out_grad.shape
+    nz, ny, nx = sizes["z"], sizes["y"], sizes["x"]
+    most = max(sizes.values()) - 1
+    count = len(GATHER_ORDERS)
+    bf16 = jnp.bfloat16
+    return pl.pallas_call(
+        functools.partial(scatter_kernel, sizes),
+        out_shape=jax.ShapeDtypeStruct((rows, width), bf16),
+        in_specs=[VMEM_SPEC] * 4,
+        out_specs=VMEM_SPEC,
+        scratch_shapes=[
+            pltpu.VMEM((nz, ny, nx, rows, width), bf16),
+            pltpu.VMEM((nz, ny, nx, rows, width), bf16),
+            pltpu.VMEM((nx - 1, nz, ny, 1, rows, width), bf16),
+            pltpu.VMEM((ny - 1, nz, 1, nx, rows, width), bf16),
+            pltpu.VMEM((nz - 1, 1, ny, nx, rows, width), bf16),
+            pltpu.VMEM((rows, width), jnp.float32),
+            pltpu.SemaphoreType.DMA((count, 4, most)),
+            pltpu.SemaphoreType.DMA((count, 4, most)),
+        ],
+        compiler_params=pltpu.CompilerParams(collective_id=1, has_side_effects=True),
+    )(part, out_grad, norm_input, norm_gain)
+
+
+def attn_kernel(
+    sizes,
+    resid_ref,
+    proj_ref,
+    attn_ref,
+    cols_ref,
+    part_ref,
+    acc_ref,
+    from_core,
+    from_y,
+    from_z,
+    col_send,
+    col_recv,
+    send_sem,
+    recv_sem,
+):
+    at = place()
+    nz, ny, nc, nx = sizes["z"], sizes["y"], sizes["c"], sizes["x"]
+    expert_count = nz * ny * nc
+    total = expert_count * nx
+    expert, half = lax.axis_index("expert"), at["x"]
+    rows, share = cols_ref.shape[1], cols_ref.shape[2]
+    me = expert * nx + half
+    barrier = pltpu.get_barrier_semaphore()
+
+    def other(step):
+        number = lax.rem(me + step, total)
+        return number // nx, lax.rem(number, nx)
+
+    def signal(step, carry):
+        to, to_half = other(step)
+        pl.semaphore_signal(
+            barrier,
+            inc=1,
+            device_id={"expert": to, "tensor": to_half},
+            device_id_type=MESH_ID,
+        )
+        return carry
+
+    lax.fori_loop(1, total, signal, 0)
+    pl.semaphore_wait(barrier, total - 1)
+
+    def column_copy(step):
+        to, to_half = other(step)
+        return pltpu.make_async_remote_copy(
+            src_ref=resid_ref.at[:, pl.ds(pl.multiple_of(to * share, share), share)],
+            dst_ref=cols_ref.at[me],
+            send_sem=col_send.at[step],
+            recv_sem=col_recv.at[step],
+            device_id={"expert": to, "tensor": to_half},
+            device_id_type=MESH_ID,
+        )
+
+    def start_columns(step, carry):
+        column_copy(step).start()
+        return carry
+
+    def wait_columns(step, carry):
+        column_copy(step).wait()
+        return carry
+
+    lax.fori_loop(1, total, start_columns, 0)
+    own = pltpu.make_async_copy(
+        resid_ref.at[:, pl.ds(pl.multiple_of(expert * share, share), share)],
+        cols_ref.at[me],
+        col_send.at[0],
+    )
+    own.start()
+    own.wait()
+    lax.fori_loop(1, total, wait_columns, 0)
+
+    wanted = cols_ref[...].reshape(total * rows, share)
+    chunks = column_chunks(proj_ref.shape[0], ATTN_CHUNKS)
+    everything = []
+
+    def send(source, target, axis, step, chunk, number):
+        copy = pltpu.make_async_remote_copy(
+            src_ref=source,
+            dst_ref=target,
+            send_sem=send_sem.at[chunk, number, step - 1],
+            recv_sem=recv_sem.at[chunk, number, step - 1],
+            device_id=device_at(moved(at, axis, step, sizes)),
+            device_id_type=MESH_ID,
+        )
+        copy.start()
+        everything.append(copy)
+        return copy
+
+    pending = {}
+    for chunk, (start, width) in enumerate(chunks):
+        cols = pl.ds(start, width)
+        product = lax.dot_general(
+            wanted,
+            proj_ref[cols, :],
+            (((1,), (1,)), ((), ())),
+            preferred_element_type=jnp.float32,
+        ).astype(jnp.bfloat16)
+        part_ref[:, :, :, :, cols] = product.reshape(nz, ny, nc, nx * rows, width)
+        pending[chunk] = [
+            send(
+                part_ref.at[:, :, 1 - at["c"], :, cols],
+                from_core.at[:, :, :, cols],
+                "c",
+                1,
+                chunk,
+                0,
+            )
+        ]
+    for chunk, (start, width) in enumerate(chunks):
+        cols = pl.ds(start, width)
+        pending[chunk][0].wait_recv()
+        acc_ref[:, :, :, cols] = added(
+            part_ref[:, :, at["c"], :, cols], from_core[:, :, :, cols]
+        )
+        pending[chunk] = [
+            send(
+                acc_ref.at[:, 1 - at["y"], :, cols],
+                from_y.at[:, :, cols],
+                "y",
+                1,
+                chunk,
+                1,
+            )
+        ]
+    for chunk, (start, width) in enumerate(chunks):
+        cols = pl.ds(start, width)
+        pending[chunk][0].wait_recv()
+        acc_ref[:, at["y"], :, cols] = added(
+            acc_ref[:, at["y"], :, cols], from_y[:, :, cols]
+        )
+        pending[chunk] = []
+        for step in range(1, nz):
+            to = moved(at, "z", step, sizes)
+            pending[chunk].append(
+                send(
+                    acc_ref.at[to["z"], at["y"], :, cols],
+                    from_z.at[step - 1, :, cols],
+                    "z",
+                    step,
+                    chunk,
+                    2,
+                )
+            )
+    for chunk, (start, width) in enumerate(chunks):
+        cols = pl.ds(start, width)
+        sum_all = acc_ref[at["z"], at["y"], :, cols].astype(jnp.float32)
+        for step in range(1, nz):
+            pending[chunk][step - 1].wait_recv()
+            sum_all = sum_all + from_z[step - 1, :, cols].astype(jnp.float32)
+        attn_ref[:, cols] = sum_all.astype(jnp.bfloat16)
+    for copy in everything:
+        copy.wait_send()
+
+
+ATTN_CHUNKS = 4
+
+
+def attn_all(resid, proj, sizes):
+    nz, ny, nc, nx = sizes["z"], sizes["y"], sizes["c"], sizes["x"]
+    rows = resid.shape[0]
+    width, share = proj.shape
+    total = nz * ny * nc * nx
+    most = max(sizes.values()) - 1
+    bf16 = jnp.bfloat16
+    return pl.pallas_call(
+        functools.partial(attn_kernel, sizes),
+        out_shape=jax.ShapeDtypeStruct((rows * nx, width), bf16),
+        in_specs=[VMEM_SPEC] * 2,
+        out_specs=VMEM_SPEC,
+        scratch_shapes=[
+            pltpu.VMEM((total, rows, share), bf16),
+            pltpu.VMEM((nz, ny, nc, nx * rows, width), bf16),
+            pltpu.VMEM((nz, ny, nx * rows, width), bf16),
+            pltpu.VMEM((nz, ny, nx * rows, width), bf16),
+            pltpu.VMEM((nz, nx * rows, width), bf16),
+            pltpu.VMEM((nz - 1, nx * rows, width), bf16),
+            pltpu.SemaphoreType.DMA((total,)),
+            pltpu.SemaphoreType.DMA((total,)),
+            pltpu.SemaphoreType.DMA((ATTN_CHUNKS, 3, most)),
+            pltpu.SemaphoreType.DMA((ATTN_CHUNKS, 3, most)),
+        ],
+        compiler_params=pltpu.CompilerParams(collective_id=2, has_side_effects=True),
+    )(resid, proj)
+
+
+def split_three(values):
+    high = lax.reduce_precision(values, 8, 7)
+    middle = lax.reduce_precision(values - high, 8, 7)
+    low = lax.reduce_precision(values - high - middle, 8, 7)
+    return tuple(piece.astype(jnp.bfloat16) for piece in (high, middle, low))
+
+
 def per_device_tokens(
     out_grad,
     norm_input,
@@ -136,7 +576,6 @@
     w_down,
     out_proj,
 ):
-    everyone = ("expert", "tensor")
     expert_count = lax.axis_size("expert")
     expert = lax.axis_index("expert")
     slot_total = gate_saved.shape[1]
@@ -147,16 +586,29 @@
     contract_last = (((1,), (1,)), ((), ()))
     contract_first = (((0,), (0,)), ((), ()))
 
+    sizes = {"z": expert_count // 4, "y": 2, "c": 2, "x": lax.axis_size("tensor")}
+    own_rows = out_grad.shape[1]
+    first_row = lax.axis_index("tensor") * own_rows
+    own_routes = lax.dynamic_slice_in_dim(routes[0], first_row, own_rows, 0)
+    own_weight = lax.dynamic_slice_in_dim(route_weight[0], first_row, own_rows, 0)
     dense = jnp.sum(
         jnp.where(
-            routes[0][:, :, None] == jnp.arange(expert_count, dtype=jnp.int32)[None, None, :],
-            route_weight[0][:, :, None],
+            own_routes[:, :, None] == jnp.arange(expert_count, dtype=jnp.int32)[None, None, :],
+            own_weight[:, :, None],
             0.0,
         ),
         axis=1,
     )
-    all_dense = lax.all_gather(dense, "expert", axis=0, tiled=False)
-    weight = lax.dynamic_index_in_dim(all_dense, expert, axis=2, keepdims=False)
+    pieces = split_three(dense)
+    padding = jnp.zeros((own_rows, ROUTE_LANES - 3 * expert_count), jnp.bfloat16)
+    rows = jnp.concatenate((out_grad[0],) + pieces + (padding,), axis=1)
+    gathered = gather_all(rows, sizes).reshape(token_total, model_width + ROUTE_LANES)
+    all_grads = gathered[:, :model_width]
+    lane = jnp.arange(ROUTE_LANES, dtype=jnp.int32)
+    mine = (lax.rem(lane, expert_count) == expert) & (lane < 3 * expert_count)
+    weight = jnp.sum(
+        jnp.where(mine[None, :], gathered[:, model_width:].astype(jnp.float32), 0.0), axis=-1
+    ).reshape(expert_count, group_tokens)
     named = weight > 0.0
     before = jnp.tril(jnp.ones((group_tokens, group_tokens), jnp.float32), -1)
     rank = jnp.einsum("gt,ut->gu", named.astype(jnp.float32), before).astype(jnp.int32)
@@ -173,7 +625,6 @@
     activation = gate * sigmoid_gate
     hidden = (activation * upper).astype(jnp.bfloat16)
 
-    all_grads = lax.all_gather(out_grad[0], everyone, axis=0, tiled=True)
     token_grad = (weight.reshape(token_total, 1) * all_grads.astype(jnp.float32)).astype(
         jnp.bfloat16
     )
@@ -191,36 +642,17 @@
         up_grad, w_up[0], contract_last, preferred_element_type=jnp.float32
     )
     part_grad = part_grad.astype(jnp.bfloat16)
-    moe_grad = lax.psum_scatter(
-        part_grad, everyone, scatter_dimension=0, tiled=True
-    ).astype(jnp.float32)
     down_grad = lax.dot_general(
         hidden, token_grad, contract_first, preferred_element_type=jnp.float32
     )
     down_grad = down_grad.astype(jnp.bfloat16)[None]
-    resid_in = norm_input[0].astype(jnp.float32)
-    inv_rms = lax.rsqrt(jnp.mean(resid_in * resid_in, axis=-1, keepdims=True) + 1e-06)
-    scaled_grad = norm_gain * moe_grad
-    projection = jnp.sum(scaled_grad * resid_in, axis=-1, keepdims=True)
-    resid_grad = (
-        out_grad[0].astype(jnp.float32)
-        + inv_rms * scaled_grad
-        - inv_rms * inv_rms * inv_rms / model_width * resid_in * projection
-    )
-    resid_grad = resid_grad.astype(jnp.bfloat16)
-    own_rows = resid_grad.shape[0]
-    columns = lax.all_to_all(
-        resid_grad.reshape(own_rows, expert_count, -1),
-        "expert",
-        split_axis=1,
-        concat_axis=0,
-        tiled=True,
-    ).reshape(expert_count, own_rows, -1)
-    columns = lax.all_gather(columns, "tensor", axis=1, tiled=True).reshape(token_total, -1)
-    attn_part = lax.dot_general(
-        columns, out_proj, contract_last, preferred_element_type=jnp.float32
-    ).astype(jnp.bfloat16)
-    attn_grad = lax.psum_scatter(attn_part, "expert", scatter_dimension=0, tiled=True)
+    part_grad = part_grad.reshape(
+        sizes["z"], sizes["y"], sizes["c"], sizes["x"], own_rows, model_width
+    )
+    resid_grad = scatter_and_norm(
+        part_grad, out_grad[0], norm_input[0], norm_gain[None], sizes
+    )
+    attn_grad = attn_all(resid_grad, out_proj, sizes)
     return (resid_grad[None], attn_grad[None], down_grad)
 
 

time: 319 us -> 141 us (0.44)
  waiting for transfers between devices: 235 us -> 0 us
  Pallas kernels: 0 us -> 113 us
  blocking collectives: 39.6 us -> 0 us
  between operations: 13.9 us -> 0.81 us
  matrix products: 26.1 us -> 19 us
  local copies, waits for them, and re-layouts: 0.23 us -> 6.73 us
    reduce_scatter x2 -> x0, waiting for transfers between devices: 196 us -> none  [the longest x1 143 us: per_device_tokens(): lax.psum_scatter(part_grad, everyone, scatter_dimension=0, tiled=True)]
    pallas_call x0 -> x3, Pallas kernels: none -> 113 us  [the longest x1 42.8 us: scatter_and_norm(): pl.pallas_call(functools.partial(scatter_kernel, sizes), out_shape=jax.Sh...]
    all_gather x1 -> x0, waiting for transfers between devices: 39 us -> none  [per_device_tokens(): all_grads = lax.all_gather(out_grad[0], everyone, axis=0, tiled=True)]
    all_gather x2 -> x0, blocking collectives: 29.1 us -> none  [the longest x1 23.5 us: per_device_tokens(): all_dense = lax.all_gather(dense, 'expert', axis=0, tiled=False)]
    all_to_all x1 -> x0, blocking collectives: 10.5 us -> none  [per_device_tokens(): lax.all_to_all(resid_grad.reshape(own_rows, expert_count, -1), 'expert',...]
  transfers between devices with their start and end apart: 3 -> 0, of which waited for: 3 -> 0; matrix products, arithmetic and copies ran while one was open for 4% -> 0% of each run, Pallas kernels for 0% -> 0%
where the time goes in v2:
time: 141 us
  Pallas kernels  113 us (80%)
  matrix products  19 us (13%)
  local copies, waits for them, and re-layouts  6.73 us (5%)
    pallas_call x1, Pallas kernels, scatter_and_norm(): pl.pallas_call(functools.partial(scatter_kernel, sizes), out_shape=jax.Sh...  42.8 us
    pallas_call x1, Pallas kernels, attn_all(): pl.pallas_call(functools.partial(attn_kernel, sizes), out_shape=jax.Shape...  35.9 us
    pallas_call x1, Pallas kernels, gather_all(): pl.pallas_call(functools.partial(gather_kernel, sizes), out_shape=jax.Sha...  34.7 us
    dot_general x1, matrix products, per_device_tokens(): lax.dot_general(token_grad, w_down[0], contract_last, preferred_element_t...  6.07 us
    dot_general x1, matrix products, per_device_tokens(): lax.dot_general(hidden, token_grad, contract_first, preferred_element_typ...  4.73 us
    dot_general x1, matrix products, per_device_tokens(): lax.dot_general(up_grad, w_up[0], contract_last, preferred_element_type=j...  4.37 us
    unnamed x14, local copies, waits for them, and re-layouts  3.17 us

profile of v2, /device:TPU:0, one launch (start us, length us, event | category | flops | bytes accessed | tf_op | source)
XLA Modules:
  0.0 141.0 jit_solution(9334632495169841050)
XLA Ops:
  0.6 0.0 copy-start
  0.7 0.8 dynamic-slice_bitcast_fusion.1
  1.5 0.8 dynamic-slice_bitcast_fusion
  2.3 0.1 copy.17
  2.4 0.1 copy.16
  2.4 0.1 select_reduce_fusion.1
  2.6 1.6 %concatenate.3.x_ref = bf16[16,4224]{1,0:T(8,128)(2,1)} concatenate(bf16[16,4096]{1,0:T(8,128)(2,1)} %bitcast.36, bf16[16,16]{1,0:T(8,128)(2,1)S(1)} %get-tuple-element.5, bf16[16,16]{1,0:T(8,128)(2,1)S(1)} %get-tuple-element.4, bf16[16,16]{1,0:T(8,128)(2,1)S(1)} %get-tuple-element.3, bf16[16,80]{1,0:T(8,128)(2,1)S(1)} %broadcast_in_dim.62), dimensions={1} | concatenate | bytes 270336 | tf_op jit(solution)/shard_map/concatenate | solution.py:604
  4.2 34.7 %shard_map.130 = bf16[4,2,2,2,16,4224]{5,4,3,2,1,0:T(8,128)(2,1)} custom-call(bf16[16,4224]{1,0:T(8,128)(2,1)} %concatenate.3.x_ref), custom_call_target="tpu_custom_call" | custom-call | tf_op jit(solution)/shard_map/pallas_call | solution.py:223
  39.0 1.0 select_reduce_fusion
  40.0 0.1 gt.11
  40.1 0.2 fusion.7
  40.3 0.1 eq.46
  40.3 0.5 fusion.9
  40.9 0.0 slice-start
  40.9 0.5 fusion.10
  41.4 6.1 %fusion.4 = f32[512,512]{1,0:T(8,128)S(1)} fusion(bf16[1,512,4096]{2,1,0:T(8,128)(2,1)} %param.20, bf16[512,4224]{1,0:T(8,128)(2,1)} %bitcast.31, f32[512]{0:T(512)S(1)} %select_reduce_fusion), kind=kOutput, calls=%fused_computation.7 | convolution fusion | flops 2153775104 | bytes 9439232 | tf_op jit(solution)/shard_map/dot_general | solution.py:631
  47.5 0.0 copy-start.1
  47.5 4.7 %fusion = bf16[1,512,4096]{2,1,0:T(8,128)(2,1)} fusion(bf16[512,4224]{1,0:T(8,128)(2,1)S(1)} %bitcast.34, f32[512]{0:T(512)S(1)} %select_reduce_fusion, f32[512,512]{1,0:T(8,128)S(1)} %fusion.10, f32[512,512]{1,0:T(8,128)S(1)} %fusion.9), kind=kOutput, calls=%fused_computation.3 | convolution fusion | flops 2157445120 | bytes 10487808 | tf_op jit(solution)/shard_map/dot_general | solution.py:645
  52.2 2.6 %fusion.2 = f32[512,4096]{1,0:T(8,128)S(1)} fusion(bf16[1,4096,512]{2,1,0:T(8,128)(2,1)S(1)} %copy-done.1, f32[512,512]{1,0:T(8,128)S(1)} %fusion.9, f32[512,512]{1,0:T(8,128)S(1)} %fusion.4, f32[512,512]{1,0:T(8,128)S(1)} %fusion.10), kind=kOutput, calls=%fused_computation.5 | convolution fusion | flops 2150105088 | bytes 15728640 | tf_op jit(solution)/shard_map/dot_general | solution.py:638
  54.9 4.4 %add_convert_fusion = bf16[512,4096]{1,0:T(8,128)(2,1)} fusion(f32[512,4096]{1,0:T(8,128)S(1)} %fusion.2, bf16[1,4096,512]{2,1,0:T(8,128)(2,1)S(1)} %copy-done.2, f32[512,512]{1,0:T(8,128)S(1)} %fusion.4, f32[512,512]{1,0:T(8,128)S(1)} %fusion.9), kind=kOutput, calls=%fused_computation | convolution fusion | flops 2153250816 | bytes 18874368 | tf_op jit(solution)/shard_map/dot_general | solution.py:641
  59.2 42.8 %shard_map.131.resid_ref = bf16[16,4096]{1,0:T(8,128)(2,1)} custom-call(bf16[4,2,2,2,16,4096]{5,4,3,2,1,0:T(8,128)(2,1)} %bitcast.29, bf16[16,4096]{1,0:T(8,128)(2,1)} %bitcast.37, bf16[16,4096]{1,0:T(8,128)(2,1)} %bitcast.39, f32[1,4096]{1,0:T(1,128)} %bitcast.40), custom_call_target="tpu_custom_call" | custom-call | tf_op jit(solution)/shard_map/pallas_call | solution.py:355
  102.0 35.9 %shard_map.132 = bf16[32,2048]{1,0:T(8,128)(2,1)} custom-call(bf16[16,4096]{1,0:T(8,128)(2,1)} %shard_map.131.resid_ref, bf16[2048,256]{1,0:T(8,128)(2,1)} %proj_ref.1), custom_call_target="tpu_custom_call" | custom-call | tf_op jit(solution)/shard_map/pallas_call | solution.py:538
  137.9 1.6 %copy.20 = bf16[1,16,4096]{2,1,0:T(8,128)(2,1)} copy(bf16[1,16,4096]{2,1,0:T(8,128)(2,1)} %bitcast.35) | data formatting | bytes 262144
  139.5 1.6 %copy.21 = bf16[1,32,2048]{2,1,0:T(8,128)(2,1)} copy(bf16[1,32,2048]{2,1,0:T(8,128)(2,1)} %bitcast.38) | data formatting | bytes 262144
  (16 shorter events, 0.1 us)
Async XLA Ops:
  0.6 39.7 %copy-start = (bf16[1,512,512]{2,1,0:T(8,128)(2,1)S(1)}, bf16[1,512,512]{2,1,0:T(8,128)(2,1)}, u32[]{:S(2)}) copy-start(bf16[1,512,512]{2,1,0:T(8,128)(2,1)} %param.16) | copy-start | bytes 1572868
  0.6 40.2 %copy-start.3 = (bf16[1,512,512]{2,1,0:T(8,128)(2,1)S(1)}, bf16[1,512,512]{2,1,0:T(8,128)(2,1)}, u32[]{:S(2)}) copy-start(bf16[1,512,512]{2,1,0:T(8,128)(2,1)} %param.17) | copy-start | bytes 1572868
  40.9 6.6 %slice-start = ((s8[4325376]{0:T(1024)(128)(4,1)}), s8[4194304]{0:T(1024)(128)(4,1)S(1)}, s32[]{:S(2)}) async-start(s8[4325376]{0:T(1024)(128)(4,1)} %bitcast.32), calls=%async_computation | async-start | bytes 8388608
  41.4 6.1 %slice-start.1 = ((s8[4325376]{0:T(1024)(128)(4,1)}), s8[131072]{0:T(1024)(128)(4,1)S(1)}, s32[]{:S(2)}) async-start(s8[4325376]{0:T(1024)(128)(4,1)} %bitcast.32), calls=%async_computation.1 | async-start | bytes 262144
  47.5 4.7 %copy-start.1 = (bf16[1,4096,512]{2,1,0:T(8,128)(2,1)S(1)}, bf16[1,4096,512]{2,1,0:T(8,128)(2,1)}, u32[]{:S(2)}) copy-start(bf16[1,4096,512]{2,1,0:T(8,128)(2,1)} %param.18) | copy-start | bytes 12582916
  52.2 2.6 %copy-start.2 = (bf16[1,4096,512]{2,1,0:T(8,128)(2,1)S(1)}, bf16[1,4096,512]{2,1,0:T(8,128)(2,1)}, u32[]{:S(2)}) copy-start(bf16[1,4096,512]{2,1,0:T(8,128)(2,1)} %param.19) | copy-start | bytes 12582916

commit v3 on v2

--- a/solution.py
+++ b/solution.py
@@ -128,7 +128,8 @@
 
 MESH_ID = pl.DeviceIdType.MESH
 ROUTE_LANES = 128
-GATHER_ORDERS = (("z", "y", "x"), ("z", "x", "y"), ("x", "z", "y"), ("y", "z", "x"))
+GATHER_ORDERS = (("z", "y", "x"), ("z", "x", "y"), ("x", "z", "y"), ("y", "z", "x")) * 2
+CHUNK_SHARES = (5, 5, 3, 3) * 2
 VMEM_SPEC = pl.BlockSpec(memory_space=pltpu.VMEM)
 
 
@@ -165,15 +166,45 @@
     pl.semaphore_wait(barrier, count)
 
 
-def column_chunks(width, count):
-    tiles = width // 128
-    edges = [tiles * i // count * 128 for i in range(count + 1)]
-    return [(edges[i], edges[i + 1] - edges[i]) for i in range(count)]
+def column_chunks(width, shares):
+    tiles, whole = width // 128, sum(shares)
+    edges = [tiles * sum(shares[:i]) // whole * 128 for i in range(len(shares) + 1)]
+    return [(edges[i], edges[i + 1] - edges[i]) for i in range(len(shares))]
+
+
+def finishing_order(sizes, orders, widths, gathers):
+    free = {axis: 0.0 for axis in "zyxc"}
+    events, done = [], []
+    blocks = sizes["z"] * sizes["y"] * sizes["x"]
+
+    def launch(now, chunk, stage, held):
+        axis = orders[chunk][stage]
+        count = sizes[axis]
+        sent = held if gathers else held / count
+        load = sent * widths[chunk] * {"z": 8.0, "y": 2.0, "x": 2.0, "c": 0.25}[axis]
+        free[axis] = max(free[axis], now) + load
+        left = held * count if gathers else held / count
+        events.append((free[axis] + LATENCY, chunk, stage, left))
+
+    for chunk in range(len(orders)):
+        launch(0.0, chunk, 0, 1 if gathers else 2 * blocks)
+    while events:
+        event = min(events)
+        events.remove(event)
+        now, chunk, stage, held = event
+        done.append((chunk, stage))
+        if stage + 1 < len(orders[chunk]):
+            launch(now, chunk, stage + 1, held)
+    return done
+
+
+LATENCY = 4000.0
 
 
 def gather_kernel(sizes, x_ref, out_ref, own_sem, send_sem, recv_sem):
     at = place()
-    chunks = column_chunks(x_ref.shape[1], len(GATHER_ORDERS))
+    chunks = column_chunks(x_ref.shape[1], CHUNK_SHARES)
+    orders = [order + ("c",) for order in GATHER_ORDERS]
     own = pltpu.make_async_copy(
         x_ref, out_ref.at[at["z"], at["y"], at["c"], at["x"]], own_sem
     )
@@ -200,18 +231,21 @@
             copies.append(copy)
         return copies
 
-    pending = {}
-    everything = []
-    for number in range(4):
-        for chunk, order in enumerate(GATHER_ORDERS):
-            full = order + ("c",)
-            for copy in pending.get(chunk, ()):
-                copy.wait_recv()
-            pending[chunk] = stage(chunk, number, full[number], full[:number])
-            everything += pending[chunk]
-    for chunk in range(len(GATHER_ORDERS)):
+    pending, everything = {}, []
+
+    def begin(chunk, number):
+        order = orders[chunk]
+        pending[chunk] = stage(chunk, number, order[number], order[:number])
+        everything.extend(pending[chunk])
+
+    for chunk in range(len(chunks)):
+        begin(chunk, 0)
+    widths = [width for _, width in chunks]
+    for chunk, number in finishing_order(sizes, orders, widths, True):
         for copy in pending[chunk]:
             copy.wait_recv()
+        if number < 3:
+            begin(chunk, number + 1)
     for copy in everything:
         copy.wait_send()
 
@@ -256,7 +290,8 @@
 ):
     at = place()
     width_all = part_ref.shape[-1]
-    chunks = column_chunks(width_all, len(GATHER_ORDERS))
+    chunks = column_chunks(width_all, CHUNK_SHARES)
+    orders = [("c",) + order[::-1] for order in GATHER_ORDERS]
     landing = {"x": from_x, "y": from_y, "z": from_z}
     greet(at, sizes, "zyxc")
     everything = []
@@ -287,51 +322,52 @@
                 0,
             )
         ]
-    for number in range(1, 5):
-        for chunk, (start, width) in enumerate(chunks):
-            cols = pl.ds(start, width)
-            order = GATHER_ORDERS[chunk][::-1]
-            for copy in pending[chunk]:
-                copy.wait_recv()
-            if number == 1:
-                for z in range(sizes["z"]):
-                    acc_ref[z, :, :, :, cols] = added(
-                        part_ref[z, :, at["c"], :, :, cols], from_core[z, :, :, :, cols]
+    widths = [width for _, width in chunks]
+    for chunk, ended in finishing_order(sizes, orders, widths, False):
+        number = ended + 1
+        cols = pl.ds(*chunks[chunk])
+        order = orders[chunk][1:]
+        for copy in pending[chunk]:
+            copy.wait_recv()
+        if number == 1:
+            for z in range(sizes["z"]):
+                acc_ref[z, :, :, :, cols] = added(
+                    part_ref[z, :, at["c"], :, :, cols], from_core[z, :, :, :, cols]
+                )
+        else:
+            axis, left = order[number - 2], order[number - 1:]
+            where = tuple(slice(None) if n in left else at[n] for n in "zyx")
+            total = acc_ref[where + (slice(None), cols)].astype(jnp.float32)
+            for step in range(1, sizes[axis]):
+                index = (step - 1,) + tuple(
+                    slice(None) if n in left else 0 for n in "zyx"
+                )
+                total = total + landing[axis][index + (slice(None), cols)].astype(
+                    jnp.float32
+                )
+            if number == 4:
+                moe_ref[:, cols] = total
+            else:
+                acc_ref[where + (slice(None), cols)] = total.astype(jnp.bfloat16)
+        if number < 4:
+            axis, left = order[number - 1], order[number:]
+            pending[chunk] = []
+            for step in range(1, sizes[axis]):
+                to = moved(at, axis, step, sizes)
+                source = tuple(slice(None) if n in left else to[n] for n in "zyx")
+                target = (step - 1,) + tuple(
+                    slice(None) if n in left else 0 for n in "zyx"
+                )
+                pending[chunk].append(
+                    send(
+                        acc_ref.at[source + (slice(None), cols)],
+                        landing[axis].at[target + (slice(None), cols)],
+                        axis,
+                        step,
+                        chunk,
+                        number,
                     )
-            else:
-                axis, left = order[number - 2], order[number - 1:]
-                where = tuple(slice(None) if n in left else at[n] for n in "zyx")
-                total = acc_ref[where + (slice(None), cols)].astype(jnp.float32)
-                for step in range(1, sizes[axis]):
-                    index = (step - 1,) + tuple(
-                        slice(None) if n in left else 0 for n in "zyx"
-                    )
-                    total = total + landing[axis][index + (slice(None), cols)].astype(
-                        jnp.float32
-                    )
-                if number == 4:
-                    moe_ref[:, cols] = total
-                else:
-                    acc_ref[where + (slice(None), cols)] = total.astype(jnp.bfloat16)
-            if number < 4:
-                axis, left = order[number - 1], order[number:]
-                pending[chunk] = []
-                for step in range(1, sizes[axis]):
-                    to = moved(at, axis, step, sizes)
-                    source = tuple(slice(None) if n in left else to[n] for n in "zyx")
-                    target = (step - 1,) + tuple(
-                        slice(None) if n in left else 0 for n in "zyx"
-                    )
-                    pending[chunk].append(
-                        send(
-                            acc_ref.at[source + (slice(None), cols)],
-                            landing[axis].at[target + (slice(None), cols)],
-                            axis,
-                            step,
-                            chunk,
-                            number,
-                        )
-                    )
+                )
     resid_in = norm_input_ref[...].astype(jnp.float32)
     inv_rms = lax.rsqrt(jnp.mean(resid_in * resid_in, axis=-1, keepdims=True) + 1e-06)
     scaled_grad = norm_gain_ref[...] * moe_ref[...]
@@ -443,7 +479,7 @@
     lax.fori_loop(1, total, wait_columns, 0)
 
     wanted = cols_ref[...].reshape(total * rows, share)
-    chunks = column_chunks(proj_ref.shape[0], ATTN_CHUNKS)
+    chunks = column_chunks(proj_ref.shape[0], (1,) * ATTN_CHUNKS)
     everything = []
 
     def send(source, target, axis, step, chunk, number):
@@ -525,7 +561,7 @@
         copy.wait_send()
 
 
-ATTN_CHUNKS = 4
+ATTN_CHUNKS = 8
 
 
 def attn_all(resid, proj, sizes):

time: 141 us -> 133 us (0.943)
  Pallas kernels: 113 us -> 106 us
    pallas_call x1, Pallas kernels: 42.8 us -> 35 us  [scatter_and_norm(): pl.pallas_call(functools.partial(scatter_kernel, sizes), out_shape=jax.Sh...]
where the time goes in v3:
time: 133 us
  Pallas kernels  106 us (80%)
  matrix products  19 us (14%)
  local copies, waits for them, and re-layouts  6.73 us (5%)
    pallas_call x1, Pallas kernels, gather_all(): pl.pallas_call(functools.partial(gather_kernel, sizes), out_shape=jax.Sha...  35.5 us
    pallas_call x1, Pallas kernels, attn_all(): pl.pallas_call(functools.partial(attn_kernel, sizes), out_shape=jax.Shape...  35.1 us
    pallas_call x1, Pallas kernels, scatter_and_norm(): pl.pallas_call(functools.partial(scatter_kernel, sizes), out_shape=jax.Sh...  35 us
    dot_general x1, matrix products, per_device_tokens(): lax.dot_general(token_grad, w_down[0], contract_last, preferred_element_t...  6.07 us
    dot_general x1, matrix products, per_device_tokens(): lax.dot_general(hidden, token_grad, contract_first, preferred_element_typ...  4.73 us
    dot_general x1, matrix products, per_device_tokens(): lax.dot_general(up_grad, w_up[0], contract_last, preferred_element_type=j...  4.37 us
    unnamed x14, local copies, waits for them, and re-layouts  3.17 us

profile of v3, /device:TPU:0, one launch (start us, length us, event | category | flops | bytes accessed | tf_op | source)
XLA Modules:
  0.0 133.2 jit_solution(349486709103152267)
XLA Ops:
  0.6 0.0 copy-start
  0.7 0.8 dynamic-slice_bitcast_fusion.1
  1.5 0.8 dynamic-slice_bitcast_fusion
  2.3 0.1 copy.17
  2.4 0.1 copy.16
  2.4 0.1 select_reduce_fusion.1
  2.6 1.6 %concatenate.3.x_ref = bf16[16,4224]{1,0:T(8,128)(2,1)} concatenate(bf16[16,4096]{1,0:T(8,128)(2,1)} %bitcast.36, bf16[16,16]{1,0:T(8,128)(2,1)S(1)} %get-tuple-element.5, bf16[16,16]{1,0:T(8,128)(2,1)S(1)} %get-tuple-element.4, bf16[16,16]{1,0:T(8,128)(2,1)S(1)} %get-tuple-element.3, bf16[16,80]{1,0:T(8,128)(2,1)S(1)} %broadcast_in_dim.62), dimensions={1} | concatenate | bytes 270336 | tf_op jit(solution)/shard_map/concatenate | solution.py:640
  4.2 35.5 %shard_map.130 = bf16[4,2,2,2,16,4224]{5,4,3,2,1,0:T(8,128)(2,1)} custom-call(bf16[16,4224]{1,0:T(8,128)(2,1)} %concatenate.3.x_ref), custom_call_target="tpu_custom_call" | custom-call | tf_op jit(solution)/shard_map/pallas_call | solution.py:257
  39.8 1.0 select_reduce_fusion
  40.8 0.1 gt.11
  40.9 0.2 fusion.7
  41.1 0.1 eq.46
  41.2 0.5 fusion.9
  41.7 0.0 slice-start
  41.7 0.5 fusion.10
  42.2 6.1 %fusion.4 = f32[512,512]{1,0:T(8,128)S(1)} fusion(bf16[1,512,4096]{2,1,0:T(8,128)(2,1)} %param.20, bf16[512,4224]{1,0:T(8,128)(2,1)} %bitcast.31, f32[512]{0:T(512)S(1)} %select_reduce_fusion), kind=kOutput, calls=%fused_computation.7 | convolution fusion | flops 2153775104 | bytes 9439232 | tf_op jit(solution)/shard_map/dot_general | solution.py:667
  48.3 0.0 copy-start.1
  48.3 4.7 %fusion = bf16[1,512,4096]{2,1,0:T(8,128)(2,1)} fusion(bf16[512,4224]{1,0:T(8,128)(2,1)S(1)} %bitcast.34, f32[512]{0:T(512)S(1)} %select_reduce_fusion, f32[512,512]{1,0:T(8,128)S(1)} %fusion.10, f32[512,512]{1,0:T(8,128)S(1)} %fusion.9), kind=kOutput, calls=%fused_computation.3 | convolution fusion | flops 2157445120 | bytes 10487808 | tf_op jit(solution)/shard_map/dot_general | solution.py:681
  53.0 2.6 %fusion.2 = f32[512,4096]{1,0:T(8,128)S(1)} fusion(bf16[1,4096,512]{2,1,0:T(8,128)(2,1)S(1)} %copy-done.1, f32[512,512]{1,0:T(8,128)S(1)} %fusion.9, f32[512,512]{1,0:T(8,128)S(1)} %fusion.4, f32[512,512]{1,0:T(8,128)S(1)} %fusion.10), kind=kOutput, calls=%fused_computation.5 | convolution fusion | flops 2150105088 | bytes 15728640 | tf_op jit(solution)/shard_map/dot_general | solution.py:674
  55.7 4.4 %add_convert_fusion = bf16[512,4096]{1,0:T(8,128)(2,1)} fusion(f32[512,4096]{1,0:T(8,128)S(1)} %fusion.2, bf16[1,4096,512]{2,1,0:T(8,128)(2,1)S(1)} %copy-done.2, f32[512,512]{1,0:T(8,128)S(1)} %fusion.4, f32[512,512]{1,0:T(8,128)S(1)} %fusion.9), kind=kOutput, calls=%fused_computation | convolution fusion | flops 2153250816 | bytes 18874368 | tf_op jit(solution)/shard_map/dot_general | solution.py:677
  60.0 35.0 %shard_map.131.resid_ref = bf16[16,4096]{1,0:T(8,128)(2,1)} custom-call(bf16[4,2,2,2,16,4096]{5,4,3,2,1,0:T(8,128)(2,1)} %bitcast.29, bf16[16,4096]{1,0:T(8,128)(2,1)} %bitcast.37, bf16[16,4096]{1,0:T(8,128)(2,1)} %bitcast.39, f32[1,4096]{1,0:T(1,128)} %bitcast.40), custom_call_target="tpu_custom_call" | custom-call | tf_op jit(solution)/shard_map/pallas_call | solution.py:391
  95.0 35.1 %shard_map.132 = bf16[32,2048]{1,0:T(8,128)(2,1)} custom-call(bf16[16,4096]{1,0:T(8,128)(2,1)} %shard_map.131.resid_ref, bf16[2048,256]{1,0:T(8,128)(2,1)} %proj_ref.1), custom_call_target="tpu_custom_call" | custom-call | tf_op jit(solution)/shard_map/pallas_call | solution.py:574
  130.1 1.6 %copy.20 = bf16[1,16,4096]{2,1,0:T(8,128)(2,1)} copy(bf16[1,16,4096]{2,1,0:T(8,128)(2,1)} %bitcast.35) | data formatting | bytes 262144
  131.7 1.6 %copy.21 = bf16[1,32,2048]{2,1,0:T(8,128)(2,1)} copy(bf16[1,32,2048]{2,1,0:T(8,128)(2,1)} %bitcast.38) | data formatting | bytes 262144
  (16 shorter events, 0.1 us)
Async XLA Ops:
  0.6 40.5 %copy-start = (bf16[1,512,512]{2,1,0:T(8,128)(2,1)S(1)}, bf16[1,512,512]{2,1,0:T(8,128)(2,1)}, u32[]{:S(2)}) copy-start(bf16[1,512,512]{2,1,0:T(8,128)(2,1)} %param.16) | copy-start | bytes 1572868
  0.6 41.0 %copy-start.3 = (bf16[1,512,512]{2,1,0:T(8,128)(2,1)S(1)}, bf16[1,512,512]{2,1,0:T(8,128)(2,1)}, u32[]{:S(2)}) copy-start(bf16[1,512,512]{2,1,0:T(8,128)(2,1)} %param.17) | copy-start | bytes 1572868
  41.7 6.6 %slice-start = ((s8[4325376]{0:T(1024)(128)(4,1)}), s8[4194304]{0:T(1024)(128)(4,1)S(1)}, s32[]{:S(2)}) async-start(s8[4325376]{0:T(1024)(128)(4,1)} %bitcast.32), calls=%async_computation | async-start | bytes 8388608
  42.2 6.1 %slice-start.1 = ((s8[4325376]{0:T(1024)(128)(4,1)}), s8[131072]{0:T(1024)(128)(4,1)S(1)}, s32[]{:S(2)}) async-start(s8[4325376]{0:T(1024)(128)(4,1)} %bitcast.32), calls=%async_computation.1 | async-start | bytes 262144
  48.3 4.7 %copy-start.1 = (bf16[1,4096,512]{2,1,0:T(8,128)(2,1)S(1)}, bf16[1,4096,512]{2,1,0:T(8,128)(2,1)}, u32[]{:S(2)}) copy-start(bf16[1,4096,512]{2,1,0:T(8,128)(2,1)} %param.18) | copy-start | bytes 12582916
  53.0 2.6 %copy-start.2 = (bf16[1,4096,512]{2,1,0:T(8,128)(2,1)S(1)}, bf16[1,4096,512]{2,1,0:T(8,128)(2,1)}, u32[]{:S(2)}) copy-start(bf16[1,4096,512]{2,1,0:T(8,128)(2,1)} %param.19) | copy-start | bytes 12582916
